TPU v7x, 128 devices: a whole 4x4x4 slice. The times are simulated.
128 devices in a mesh: facet: 32 (over z, y_hi, x), freq: 4 (over y_lo, core).
Axes of the slice: x: 4, y: 4 (y_hi: 2, y_lo: 2; y = y_hi * 2 + y_lo), z: 4, core: 2. Of those that a mesh axis runs over, the one named last changes fastest.
Arguments:
- visibilities: float32 [32, 10, 2, 128, 128], P('facet', None, None, 'freq'), may hold values from -6 to 6
- coords: float32 [32, 10, 3, 128], P('facet'), may hold values from -1500 to 1500, as said below
- corners: int32 [2, 32, 10], replicated, may hold values from 0 to 480
- owners: int32 [2], replicated, may hold values from 0 to 31, as said below
- assign: int32 [32, 20], P('facet'), may hold values from 0 to 19, as said below
- counts: int32 [32], P('facet'), may hold values from 2 to 20, as said below
Outputs:
- dirty: float32 [32, 512, 512], P('facet', 'freq')
Inputs may be any that keep to these rules, and one draw needn't show every extreme that they name: `owners`: the two sets lie in different slots, one of them in the last slot. `assign`: each facet's row is a permutation of the 20 block numbers; only its first counts entries are gridded. `counts`: some facet grids all 20 blocks. `coords`: at every channel, u and v of each row of a block lie within 12 cells of the centre of that block's subgrid.
All inputs are finite; a program needn't handle non-finite values.
Results may differ from a plain program's by a relative error of at most 0.0037.
Values sent between devices are 32-bit elements; how exact they have to be, the bound alone decides.
A program may use at most 64 MiB of HBM per device.

v0:
```python
import functools
import math

import jax
import jax.numpy as jnp
import numpy as np
from jax import lax
from jax.experimental import pallas as pl
from jax.experimental.pallas import tpu as pltpu
from jax.sharding import PartitionSpec as P

SUB = 32
G = 512
BPC = 10
CH = 32
N_FACET = 32
N_FREQ = 4
BLK = 128
CHANS = CH * N_FREQ
CHUNK = 8
LO = True
MESH = pl.DeviceIdType.MESH
f32 = jnp.float32
bf16 = jnp.bfloat16

DELTA = (
    (0, 0, 0),
    (1, 0, 0),
    (3, 0, 0),
    (0, 0, 1),
    (0, 0, 3),
    (1, 0, 1),
    (1, 0, 3),
    (3, 0, 1),
    (3, 0, 3),
    (0, 1, 0),
)
LAST = N_FACET - 1
PER_SET = 3
SLOTS = 2 * PER_SET


def fit_sincos():
    s = 0.125 * (1.0 - np.cos(np.pi * (np.arange(400) + 0.5) / 400))
    t = np.sqrt(s)
    poly = np.polynomial.chebyshev
    domain = [0.0, 0.25]
    c = poly.Chebyshev.fit(s, np.cos(2 * np.pi * t), 7, domain=domain)
    n = poly.Chebyshev.fit(s, np.sin(2 * np.pi * t) / t, 7, domain=domain)
    to_power = lambda p: p.convert(kind=np.polynomial.Polynomial).coef
    return [float(v) for v in to_power(c)], [float(v) for v in to_power(n)]


COS_POLY, SIN_POLY = fit_sincos()


def sincos(cycles):
    t = cycles - jnp.floor(cycles + 0.5)
    s = t * t
    c = jnp.full_like(s, COS_POLY[-1])
    for k in COS_POLY[-2::-1]:
        c = c * s + k
    n = jnp.full_like(s, SIN_POLY[-1])
    for k in SIN_POLY[-2::-1]:
        n = n * s + k
    return c, n * t


def cmul(a, b):
    return a[0] * b[0] - a[1] * b[1], a[0] * b[1] + a[1] * b[0]


def both(a, b):
    rr, ii, ri, ir = a[0] * b[0], a[1] * b[1], a[0] * b[1], a[1] * b[0]
    return (rr - ii, ri + ir), (rr + ii, ir - ri)


def image_table():
    x = np.arange(G) - G // 2
    l = np.arange(SUB) - SUB // 2
    n = np.arange(SUB) - SUB // 2
    theta = x[:, None] / G - l[None, :] / SUB
    kernel = np.exp(2j * np.pi * n[None, None, :] * theta[:, :, None]).sum(axis=2)
    real = (kernel * np.exp(1j * np.pi * theta)).real
    real = real * (1.0 - 0.8 * (l / (SUB / 2.0)) ** 2)[None, :]
    upper, lower = real[:, SUB // 2 :], real[:, SUB // 2 - 1 :: -1]
    even, odd = upper + lower, upper - lower
    plain = np.concatenate([even, odd], axis=1)
    table = np.zeros((G, SUB))
    for row in range(SUB):
        m, one, two, t = row // 8, (row // 4) % 2, (row // 2) % 2, row % 2
        for s1 in (1, -1):
            for s2 in (1, -1):
                place = int(8 + s1 * (4 + s2 * (m + 0.5)) - 0.5)
                sign = {
                    (0, 0, 0): 1, (0, 1, 1): -s2, (1, 0, 1): -s1 * s2, (1, 1, 0): -s1,
                    (1, 0, 0): 1, (1, 1, 1): -s2, (0, 1, 0): s1, (0, 0, 1): s1 * s2,
                }[(one, two, t)]
                table[:, row] += sign * ((odd if (one + two + t) % 2 else even)[:, place])
    return table, plain


def shifted(f, delta, sign):
    z, y, x = f // 8, (f // 4) % 2, f % 4
    z = (z + (delta[0] if sign > 0 else 4 - delta[0])) % 4
    y = (y + delta[1]) % 2
    x = (x + (delta[2] if sign > 0 else 4 - delta[2])) % 4
    return z * 8 + y * 4 + x


def shifted_int(f, delta):
    return ((f // 8 + delta[0]) % 4) * 8 + ((f // 4 % 2 + delta[1]) % 2) * 4 + (f % 4 + delta[2]) % 4


def group_of(z, y, x):
    return (z + x + 2 * y) % N_FREQ


def group_at(f):
    return group_of(f // 8, (f // 4) % 2, f % 4)


GROUP = tuple(group_of(*d) for d in DELTA)
MEMBERS = tuple(tuple(j for j in range(BPC) if GROUP[j] == g) for g in range(N_FREQ))
RANK = tuple(MEMBERS[GROUP[j]].index(j) for j in range(BPC))
LAST_POS = tuple(shifted_int(LAST, d) for d in DELTA)


def unit_products(q, block, cand_vis, cand_coord, ou, ov, xrow, pbuf, vbuf, acc):
    step = 0.02 / CHANS
    start = 1.0 + (step * CH) * q.astype(f32)
    coord = cand_coord[block]
    u, v, w = coord[0:1, :], coord[1:2, :], coord[2:3, :]
    ou = 240.5 - ou.astype(f32)
    ov = 240.5 - ov.astype(f32)
    row = lax.broadcasted_iota(jnp.int32, (32, BLK), 0)

    def wave(d, corner, m, back=0.0):
        return sincos((d * start + corner) * m - back), sincos((d * step) * m)

    row8 = row[:8]
    x, x_turn = wave(
        u, ou, (2 * (row8 % 4) + 1).astype(f32) * (1.0 / 64.0), (row8 // 4).astype(f32) * 0.25
    )
    y, y_turn = wave(v, ov, (2 * row[:16] + 1).astype(f32) * (1.0 / 64.0))
    half, half_turn = wave(u, ou, jnp.full((8, BLK), 0.125, f32))
    a = (row % 8).astype(f32) - 3.5
    e = (row // 8).astype(f32) - 1.5
    rho = 0.0004 * (a * a + e * e)
    shift = -rho / (1.0 + jnp.sqrt(1.0 - rho))
    cycles = u * a + v * e + w * shift - (u + v) * (1.0 / 64.0)
    spin = sincos(cycles * start - (ou + ov) * (1.0 / 64.0))
    spin_turn = sincos(cycles * step)
    state = [x, y, half, spin]
    turns = [x_turn, y_turn, half_turn, spin_turn]
    rows4 = lambda t: jnp.concatenate([t] * 4, axis=0)

    def generate(c, slot, cc):
        x, y, half, spin = state
        xrow[slot, cc] = x[0]
        ys = jnp.concatenate(y, axis=0)
        for r in range(8):
            pbuf[slot, cc, r * 32 : (r + 1) * 32, :] = (
                jnp.broadcast_to(xrow[slot, cc, r : r + 1, :], (32, BLK)) * ys
            ).astype(bf16)
        re = jnp.broadcast_to(cand_vis[block, 0, c : c + 1, :], (32, BLK))
        im = jnp.broadcast_to(cand_vis[block, 1, c : c + 1, :], (32, BLK))
        rotated = cmul((re, im), spin)
        c2, s2 = half
        c1, s1 = c2 * c2 - s2 * s2, 2.0 * (c2 * s2)
        for n, factor in enumerate((c1 * c2, c1 * s2, s1 * c2, s1 * s2)):
            factor = rows4(factor)
            for part in range(2):
                value = rotated[part] * factor
                high = value.astype(bf16)
                at = n * 64 + part * 32
                vbuf[slot, cc, at : at + 32, :] = high
                if LO:
                    vbuf[slot, cc, 256 + at : 288 + at, :] = (value - high.astype(f32)).astype(bf16)
        for n in range(4):
            state[n] = cmul(state[n], turns[n])

    def multiply(k, slot):
        left = jnp.concatenate([vbuf[slot, cc] for cc in range(CHUNK)], axis=1)
        right = jnp.concatenate([pbuf[slot, cc] for cc in range(CHUNK)], axis=1)
        part = lax.dot_general(
            left, right, (((1,), (1,)), ((), ())), preferred_element_type=f32
        )
        acc[...] = part if k == 0 else acc[...] + part

    chunks = CH // CHUNK
    for k in range(chunks + 1):
        for cc in range(CHUNK):
            if k < chunks:
                generate(k * CHUNK + cc, k % 2, cc)
        if k > 0:
            multiply(k - 1, (k - 1) % 2)


def place_results(acc, turned, put):
    for n in range(4):
        for h in range(2):
            rows, lanes = slice(n * 64, (n + 1) * 64), slice(h * 128, (h + 1) * 128)
            value = acc[rows, lanes]
            if LO:
                value = value + acc[256 + n * 64 : 320 + n * 64, lanes]
            turned[(2 * n + h) * 64 : (2 * n + h + 1) * 64, :] = value
    for part in range(2):
        for facet in range(N_FACET):
            put(facet, part, turned[pl.ds(part * 32 + facet, 8, stride=64), :])


def unit_scratch():
    rows = 512 if LO else 256
    return [
        pltpu.VMEM((2, CHUNK, 8, BLK), f32),
        pltpu.VMEM((2, CHUNK, 256, BLK), bf16),
        pltpu.VMEM((2, CHUNK, rows, BLK), bf16),
        pltpu.VMEM((rows, 256), f32),
        pltpu.VMEM((512, 128), f32),
    ]


def pick(index, values):
    out = jnp.int32(values[0])
    for n, v in enumerate(values):
        if n:
            out = jnp.where(index == n, v, out)
    return out


def split(a):
    high = a.astype(bf16)
    return high, (a - high.astype(f32)).astype(bf16)


def dot3(a, b):
    dot = functools.partial(jnp.dot, preferred_element_type=f32)
    return dot(a[0], b[0]) + (dot(a[0], b[1]) + dot(a[1], b[0]))


def lanes_of(values):
    group = lax.broadcasted_iota(jnp.int32, (1, 128), 1) // 32
    tiles = []
    for tile in range(5):
        v = jnp.full((1, 128), values[tile * 4], jnp.int32)
        for g in range(1, 4):
            v = jnp.where(group == g, values[tile * 4 + g], v)
        tiles.append(v)
    return jnp.concatenate(tiles, axis=1)


def prepare_image(q, owners, corners, assign, counts, other, table_t, pre, pim, br, bi):
    first_last = owners[0] == LAST
    corner_u = [corners[0, LAST, j] for j in range(BPC)] + [corners[0, other, j] for j in range(BPC)]
    corner_v = [corners[1, LAST, j] for j in range(BPC)] + [corners[1, other, j] for j in range(BPC)]
    k_of = lax.broadcasted_iota(jnp.int32, (1, 640), 1) // 32
    block = jnp.where(first_last, k_of, jnp.where(k_of < BPC, k_of + BPC, k_of - BPC))
    weight = jnp.zeros((1, 640), f32)
    count = counts[0]
    for n in range(2 * BPC):
        live = jnp.where(n < count, 1.0, 0.0).astype(f32)
        weight = weight + jnp.where(block == assign[0, n], live, 0.0)
    rows = q * 128 - 256 + lax.broadcasted_iota(jnp.int32, (128, 640), 0)
    turns = jnp.bitwise_and(rows * (2 * lanes_of(corner_u) - 481), 1023)
    c, s = sincos(turns.astype(f32) * (1.0 / 1024.0))
    pre[...] = c * weight
    pim[...] = s * weight
    columns = lax.broadcasted_iota(jnp.int32, (1, G), 1) - 256
    for k in range(2 * BPC):
        turns = jnp.bitwise_and(columns * (2 * corner_v[k] - 481), 1023)
        c, s = sincos(turns.astype(f32) * (1.0 / 1024.0))
        for ref, value in ((br, table_t[...] * c), (bi, table_t[...] * -s)):
            high, low = split(value)
            ref[0, k * 32 : (k + 1) * 32, :] = high
            ref[1, k * 32 : (k + 1) * 32, :] = low


def make_image(q, other, got, table, pre, pim, br, bi, zr, zi, out):
    lane = lax.broadcasted_iota(jnp.int32, (8, 128), 1)
    sub = lax.broadcasted_iota(jnp.int32, (8, 128), 0)
    row_sine = (sub // 4 + (sub // 2) % 2 + sub % 2) % 2 == 1
    lane_sine = lane % 32 >= 16
    two = jnp.logical_and(row_sine, lane_sine)
    one = jnp.logical_and(jnp.logical_or(row_sine, lane_sine), jnp.logical_not(two))
    group = lane // 32
    home = group_at(other)
    for tile in range(5):
        parts = [[None] * 4, [None] * 4]
        for g in range(4):
            k = tile * 4 + g
            j = k % BPC
            if k < BPC:
                block = got[(group_at(LAST) + GROUP[j]) % N_FREQ * SLOTS + PER_SET + RANK[j]]
            else:
                block = got[(home + GROUP[j]) % N_FREQ * SLOTS + RANK[j]]
            re, im = block[:8], block[8:]
            new_re = jnp.where(one, -im, jnp.where(two, -re, re))
            new_im = jnp.where(one, re, jnp.where(two, -im, im))
            for i4 in range(4):
                shift = ((g - i4) * 32) % 128
                for p, value in enumerate((new_re, new_im)):
                    if shift:
                        value = pltpu.roll(value, shift, 1)
                    old = parts[p][i4]
                    parts[p][i4] = value if old is None else jnp.where(group == g, value, old)
        for i4 in range(4):
            zr[i4 * 8 : (i4 + 1) * 8, tile * 128 : (tile + 1) * 128] = parts[0][i4]
            zi[i4 * 8 : (i4 + 1) * 8, tile * 128 : (tile + 1) * 128] = parts[1][i4]
    d = split(table[pl.ds(pl.multiple_of(q * 128, 128), 128), :])
    t_re, t_im = dot3(d, split(zr[...])), dot3(d, split(zi[...]))
    l_re = t_re * pre[...] - t_im * pim[...]
    l_im = t_re * pim[...] + t_im * pre[...]
    out[0] = dot3(split(l_re), (br[0], br[1])) + dot3(split(l_im), (bi[0], bi[1]))


def fused_kernel(
    vis, coord, owners, corners, assign, counts, table, table_t, out,
    cand_vis, cand_coord, xrow, pbuf, vbuf, acc, turned, res, from_a, from_b, total, got,
    pre, pim, br, bi, zr, zi,
    move_send, move_recv, send_sem, recv_a, recv_b, peer_send, peer_recv,
):
    f = lax.axis_index("facet")
    q = lax.axis_index("freq")
    group = group_at(f)
    last_block = jnp.int32(-1)
    for j in range(BPC):
        last_block = jnp.where(f == LAST_POS[j], j, last_block)
    is_last = last_block >= 0
    last_rank = pick(last_block, RANK)
    other = jnp.where(owners[0] == LAST, owners[1], owners[0]).astype(jnp.int32)
    barrier = pltpu.get_barrier_semaphore()

    def signal(facet, freq):
        pl.semaphore_signal(barrier, inc=1, device_id=(facet, freq), device_id_type=MESH)

    for j in range(1, BPC):
        signal(shifted(f, DELTA[j], -1), q)

    def tell(n, carry):
        z, y, freq = n // 8, (n // 4) % 2, n % 4
        facet = z * 8 + y * 4 + (q + 8 - z - 2 * y) % 4

        @pl.when(jnp.logical_or(facet != f, freq != q))
        def _():
            signal(facet, freq)

        return carry

    lax.fori_loop(0, 32, tell, 0)
    for j in range(BPC):
        facet = LAST_POS[j]

        @pl.when(group_at(facet) == q)
        def _():
            for freq in range(N_FREQ):

                @pl.when(jnp.logical_or(f != facet, freq != q))
                def _():
                    signal(facet, freq)

    for d in range(1, N_FREQ):
        signal(f, (q + d) % N_FREQ)
    mine = jnp.where(group == q, 1, 0)
    expected = 9 + 32 + 3 - mine + jnp.where(is_last, 32 - mine, 0)
    own = [
        pltpu.make_async_copy(vis.at[0, 0], cand_vis.at[0], move_recv.at[0, 0]),
        pltpu.make_async_copy(coord.at[0, 0], cand_coord.at[0], move_recv.at[0, 1]),
    ]
    for c in own:
        c.start()
    pl.semaphore_wait(barrier, expected)
    moves = []
    for j in range(BPC - 1, 0, -1):
        to = (shifted(f, DELTA[j], 1), q)
        for n, (src, dst) in enumerate(((vis, cand_vis), (coord, cand_coord))):
            moves.append(
                pltpu.make_async_remote_copy(
                    src_ref=src.at[0, j],
                    dst_ref=dst.at[j],
                    send_sem=move_send.at[j, n],
                    recv_sem=move_recv.at[j, n],
                    device_id=to,
                    device_id_type=MESH,
                )
            )
            moves[-1].start()
    for c in own:
        c.wait()
    for c in moves:
        c.wait_recv()

    place = f // 4

    def result_copy(n, facet):
        dst, sem, at = (from_a, recv_a, place) if n == 0 else (from_b, recv_b, last_rank)
        return pltpu.make_async_remote_copy(
            src_ref=res.at[n, facet],
            dst_ref=dst.at[at, q],
            send_sem=send_sem.at[n, facet],
            recv_sem=sem.at[at, q],
            device_id=(facet, group),
            device_id_type=MESH,
        )

    def own_copy(n):
        dst, sem, at = (from_a, recv_a, place) if n == 0 else (from_b, recv_b, last_rank)
        return pltpu.make_async_copy(res.at[n, f], dst.at[at, q], sem.at[at, q])

    def send_all(n):
        def step(d, carry):
            facet = (f + d) % N_FACET
            here = jnp.logical_and(facet == f, group == q)

            @pl.when(jnp.logical_not(here))
            def _():
                result_copy(n, facet).start()

            @pl.when(here)
            def _():
                own_copy(n).start()

            return carry

        lax.fori_loop(0, N_FACET, step, 0)

    def drain(n):
        def step(facet, carry):
            @pl.when(jnp.logical_not(jnp.logical_and(facet == f, group == q)))
            def _():
                result_copy(n, facet).wait_send()

            return carry

        lax.fori_loop(0, N_FACET, step, 0)

    def unit(n, carry):
        owner = jnp.where(n == 1, LAST, other)
        block = jnp.int32(0)
        for j in range(1, BPC):
            block = jnp.where(shifted(f, DELTA[j], -1) == owner, j, block)
        unit_products(
            q, block, cand_vis, cand_coord, corners[0, owner, block], corners[1, owner, block],
            xrow, pbuf, vbuf, acc,
        )

        def put(facet, part, value):
            res[n, facet, part * 8 : (part + 1) * 8, :] = value

        place_results(acc, turned, put)

        @pl.when(n == 0)
        def _():
            send_all(0)

        @pl.when(n == 1)
        def _():
            send_all(1)

        return carry

    lax.fori_loop(0, 1 + jnp.where(is_last, 1, 0), unit, 0)

    prepare_image(q, owners, corners, assign, counts, other, table_t, pre, pim, br, bi)

    def settle(sem, dst, s):
        for p in range(N_FREQ):
            pltpu.make_async_copy(dst.at[s, p], dst.at[s, p], sem.at[s, p]).wait()

    for s in range(8):
        settle(recv_a, from_a, s)
    wanted = (q + N_FREQ - group_at(other)) % N_FREQ
    for s in range(PER_SET):
        at = jnp.int32(0)
        for g in range(N_FREQ):
            j = MEMBERS[g][min(s, len(MEMBERS[g]) - 1)]
            at = jnp.where(wanted == g, shifted(other, DELTA[j], 1) // 4, at)
        total[s] = (from_a[at, 0] + from_a[at, 1]) + (from_a[at, 2] + from_a[at, 3])
    wanted = (q + N_FREQ - group_at(LAST)) % N_FREQ
    for s in range(PER_SET):
        present = pick(wanted, [int(s < len(m)) for m in MEMBERS]) == 1

        @pl.when(present)
        def _():
            settle(recv_b, from_b, s)
            total[PER_SET + s] = (from_b[s, 0] + from_b[s, 1]) + (from_b[s, 2] + from_b[s, 3])

        @pl.when(jnp.logical_not(present))
        def _():
            total[PER_SET + s] = jnp.zeros((16, 128), f32)

    peers = []
    for d in range(1, N_FREQ):
        peers.append(
            pltpu.make_async_remote_copy(
                src_ref=total,
                dst_ref=got.at[pl.ds(q * SLOTS, SLOTS)],
                send_sem=peer_send.at[d],
                recv_sem=peer_recv.at[d],
                device_id=(f, (q + d) % N_FREQ),
                device_id_type=MESH,
            )
        )
        peers[-1].start()
    keep = pltpu.make_async_copy(total, got.at[pl.ds(q * SLOTS, SLOTS)], peer_send.at[0])
    keep.start()
    keep.wait()
    for d in range(1, N_FREQ):
        source = (q + N_FREQ - d) % N_FREQ
        pltpu.make_async_copy(total, got.at[pl.ds(source * SLOTS, SLOTS)], peer_recv.at[d]).wait()
    make_image(q, other, got, table, pre, pim, br, bi, zr, zi, out)
    for c in moves:
        c.wait_send()
    for p in peers:
        p.wait_send()
    drain(0)

    @pl.when(is_last)
    def _():
        drain(1)


def on_device(visibilities, coords, corners, owners, assign, counts):
    d, _ = image_table()
    plain = image_table()[1]
    scale = 1.0 / (SUB * SUB * math.sqrt(2 * BPC * BLK * CHANS))
    smem = pl.BlockSpec(memory_space=pltpu.SMEM)
    vmem = pl.BlockSpec(memory_space=pltpu.VMEM)
    hbm = pl.BlockSpec(memory_space=pl.ANY)
    dma = pltpu.SemaphoreType.DMA
    return pl.pallas_call(
        fused_kernel,
        out_shape=jax.ShapeDtypeStruct((1, G // N_FREQ, G), f32),
        in_specs=[hbm, hbm] + [smem] * 4 + [vmem] * 2,
        out_specs=vmem,
        scratch_shapes=[
            pltpu.VMEM((BPC, 2, CH, BLK), f32),
            pltpu.VMEM((BPC, 3, BLK), f32),
        ]
        + unit_scratch()
        + [
            pltpu.VMEM((2, N_FACET, 16, 128), f32),
            pltpu.VMEM((8, N_FREQ, 16, 128), f32),
            pltpu.VMEM((PER_SET, N_FREQ, 16, 128), f32),
            pltpu.VMEM((SLOTS, 16, 128), f32),
            pltpu.VMEM((N_FREQ * SLOTS, 16, 128), f32),
            pltpu.VMEM((128, 640), f32),
            pltpu.VMEM((128, 640), f32),
            pltpu.VMEM((2, 640, G), bf16),
            pltpu.VMEM((2, 640, G), bf16),
            pltpu.VMEM((32, 640), f32),
            pltpu.VMEM((32, 640), f32),
            dma((BPC, 2)),
            dma((BPC, 2)),
            dma((2, N_FACET)),
            dma((8, N_FREQ)),
            dma((PER_SET, N_FREQ)),
            dma((N_FREQ,)),
            dma((N_FREQ,)),
        ],
        compiler_params=pltpu.CompilerParams(collective_id=0, has_side_effects=True),
        name="grid_and_image",
    )(
        visibilities,
        coords,
        owners,
        corners,
        assign,
        counts,
        jnp.asarray(d * scale, f32),
        jnp.asarray(plain.T, f32),
    )


def solution(mesh):
    placed = (
        P("facet", None, None, "freq", None),
        P("facet", None, None, None),
        P(),
        P(),
        P("facet", None),
        P("facet"),
    )
    return jax.shard_map(
        on_device, mesh=mesh, in_specs=placed, out_specs=P("facet", "freq", None), check_vma=False
    )
```

profile of v0, /device:TPU:1, one launch (start us, length us, event | category | flops | bytes accessed | tf_op | source)
XLA Modules:
  0.0 39.6 jit_solution(15896831622301096322)
XLA Ops:
  0.7 0.0 copy-start
  0.7 1.3 %copy.9.coord = f32[1,10,3,128]{3,2,1,0:T(4,128)} copy(f32[1,10,3,128]{3,0,2,1:T(1,128)} %param.9) | data formatting | bytes 30720 | tf_op args[1]
  2.0 0.0 copy-done
  2.0 0.7 %copy.10.corners = s32[2,32,10]{2,1,0:T(8,128)} copy(s32[2,32,10]{1,0,2:T(2,128)S(1)} %copy-done) | data formatting | bytes 5120 | tf_op args[2]
  2.7 35.2 %grid_and_image.1 = f32[1,128,512]{2,1,0:T(8,128)} custom-call(f32[1,10,2,32,128]{4,3,2,1,0:T(8,128)} %vis.1, f32[1,10,3,128]{3,2,1,0:T(4,128)} %copy.9.coord, s32[2]{0:T(128)} %owners.1, s32[2,32,10]{2,1,0:T(8,128)} %copy.10.corners, s32[1,20]{1,0:T(1,128)} %assign.1, s32[1]{0:T(128)S(6)} %copy.12.counts, f32[512,32]{1,0:T(8,128)} %constant.4.clone.table, ...), custom_call_target="tpu_custom_call" | custom-call | tf_op jit(solution)/shard_map/grid_and_image/pallas_call | solution.py:531
  37.9 1.7 %copy.13 = f32[1,128,512]{2,1,0:T(8,128)} copy(f32[1,128,512]{2,1,0:T(8,128)} %grid_and_image.1) | data formatting | bytes 524288
Async XLA Ops:
  0.7 1.3 %copy-start = (s32[2,32,10]{1,0,2:T(2,128)S(1)}, s32[2,32,10]{1,0,2:T(2,128)}, u32[]{:S(2)}) copy-start(s32[2,32,10]{1,0,2:T(2,128)} %param.10) | copy-start | bytes 7684
where the time goes:
time: 39.8 us; the launch traced here: 39.6 us
  Pallas kernels  35.2 us (88%)
  local copies, waits for them, and re-layouts  3.7 us (9%)
  between operations  0.67 us (2%)
    pallas_call x1, Pallas kernels, on_device(): pl.pallas_call(fused_kernel, out_shape=jax.ShapeDtypeStruct((1, G // N_FR...  35.2 us
    unnamed x5, local copies, waits for them, and re-layouts  3.7 us

commit v1 on v0

--- a/solution.py
+++ b/solution.py
@@ -18,7 +18,7 @@
 BLK = 128
 CHANS = CH * N_FREQ
 CHUNK = 8
-LO = True
+LO = False
 MESH = pl.DeviceIdType.MESH
 f32 = jnp.float32
 bf16 = jnp.bfloat16
@@ -123,14 +123,23 @@
 GROUP = tuple(group_of(*d) for d in DELTA)
 MEMBERS = tuple(tuple(j for j in range(BPC) if GROUP[j] == g) for g in range(N_FREQ))
 RANK = tuple(MEMBERS[GROUP[j]].index(j) for j in range(BPC))
+def hops(delta):
+    return min(delta[0], 4 - delta[0]) + 2 * delta[1] + min(delta[2], 4 - delta[2])
+
+
+SEND_ORDER = tuple(
+    sorted(
+        ((n * 13 % 32 // 8, n * 13 % 32 // 4 % 2, n * 13 % 4) for n in range(1, N_FACET)),
+        key=lambda d: -hops(d),
+    )
+)
 LAST_POS = tuple(shifted_int(LAST, d) for d in DELTA)
 
 
 def unit_products(q, block, cand_vis, cand_coord, ou, ov, xrow, pbuf, vbuf, acc):
     step = 0.02 / CHANS
     start = 1.0 + (step * CH) * q.astype(f32)
-    coord = cand_coord[block]
-    u, v, w = coord[0:1, :], coord[1:2, :], coord[2:3, :]
+    u, v, w = cand_coord[3 * block], cand_coord[3 * block + 1], cand_coord[3 * block + 2]
     ou = 240.5 - ou.astype(f32)
     ov = 240.5 - ov.astype(f32)
     row = lax.broadcasted_iota(jnp.int32, (32, BLK), 0)
@@ -252,8 +261,8 @@
 
 def prepare_image(q, owners, corners, assign, counts, other, table_t, pre, pim, br, bi):
     first_last = owners[0] == LAST
-    corner_u = [corners[0, LAST, j] for j in range(BPC)] + [corners[0, other, j] for j in range(BPC)]
-    corner_v = [corners[1, LAST, j] for j in range(BPC)] + [corners[1, other, j] for j in range(BPC)]
+    corner_u = [corners[j, 0, LAST] for j in range(BPC)] + [corners[j, 0, other] for j in range(BPC)]
+    corner_v = [corners[j, 1, LAST] for j in range(BPC)] + [corners[j, 1, other] for j in range(BPC)]
     k_of = lax.broadcasted_iota(jnp.int32, (1, 640), 1) // 32
     block = jnp.where(first_last, k_of, jnp.where(k_of < BPC, k_of + BPC, k_of - BPC))
     weight = jnp.zeros((1, 640), f32)
@@ -307,8 +316,15 @@
         for i4 in range(4):
             zr[i4 * 8 : (i4 + 1) * 8, tile * 128 : (tile + 1) * 128] = parts[0][i4]
             zi[i4 * 8 : (i4 + 1) * 8, tile * 128 : (tile + 1) * 128] = parts[1][i4]
-    d = split(table[pl.ds(pl.multiple_of(q * 128, 128), 128), :])
-    t_re, t_im = dot3(d, split(zr[...])), dot3(d, split(zi[...]))
+    d = table[pl.ds(pl.multiple_of(q * 128, 128), 128), :]
+
+    def apply(z):
+        high, low = split(z)
+        return jnp.dot(
+            d, jnp.concatenate([high, low, high], axis=0), preferred_element_type=f32
+        )
+
+    t_re, t_im = apply(zr[...]), apply(zi[...])
     l_re = t_re * pre[...] - t_im * pim[...]
     l_im = t_re * pim[...] + t_im * pre[...]
     out[0] = dot3(split(l_re), (br[0], br[1])) + dot3(split(l_im), (bi[0], bi[1]))
@@ -318,7 +334,7 @@
     vis, coord, owners, corners, assign, counts, table, table_t, out,
     cand_vis, cand_coord, xrow, pbuf, vbuf, acc, turned, res, from_a, from_b, total, got,
     pre, pim, br, bi, zr, zi,
-    move_send, move_recv, send_sem, recv_a, recv_b, peer_send, peer_recv,
+    plane_sem, near_sem, all_sem, move_send, move_recv, send_sem, recv_a, recv_b, peer_send, peer_recv,
 ):
     f = lax.axis_index("facet")
     q = lax.axis_index("freq")
@@ -334,50 +350,34 @@
     def signal(facet, freq):
         pl.semaphore_signal(barrier, inc=1, device_id=(facet, freq), device_id_type=MESH)
 
+    def peers_of(n):
+        return (f, (q + n) % N_FREQ)
+
     for j in range(1, BPC):
         signal(shifted(f, DELTA[j], -1), q)
-
-    def tell(n, carry):
-        z, y, freq = n // 8, (n // 4) % 2, n % 4
-        facet = z * 8 + y * 4 + (q + 8 - z - 2 * y) % 4
-
-        @pl.when(jnp.logical_or(facet != f, freq != q))
-        def _():
-            signal(facet, freq)
-
-        return carry
-
-    lax.fori_loop(0, 32, tell, 0)
-    for j in range(BPC):
-        facet = LAST_POS[j]
-
-        @pl.when(group_at(facet) == q)
-        def _():
-            for freq in range(N_FREQ):
-
-                @pl.when(jnp.logical_or(f != facet, freq != q))
-                def _():
-                    signal(facet, freq)
-
-    for d in range(1, N_FREQ):
-        signal(f, (q + d) % N_FREQ)
-    mine = jnp.where(group == q, 1, 0)
-    expected = 9 + 32 + 3 - mine + jnp.where(is_last, 32 - mine, 0)
+    for n in range(1, N_FREQ):
+        signal(*peers_of(n))
+
+    def tell(sem, facet, freq):
+        pl.semaphore_signal(sem, inc=1, device_id=(facet, freq), device_id_type=MESH)
+
     own = [
         pltpu.make_async_copy(vis.at[0, 0], cand_vis.at[0], move_recv.at[0, 0]),
-        pltpu.make_async_copy(coord.at[0, 0], cand_coord.at[0], move_recv.at[0, 1]),
+        pltpu.make_async_copy(coord.at[pl.ds(0, 3)], cand_coord.at[pl.ds(0, 3)], move_recv.at[0, 1]),
     ]
     for c in own:
         c.start()
-    pl.semaphore_wait(barrier, expected)
+    pl.semaphore_wait(barrier, BPC - 1 + N_FREQ - 1)
     moves = []
     for j in range(BPC - 1, 0, -1):
         to = (shifted(f, DELTA[j], 1), q)
-        for n, (src, dst) in enumerate(((vis, cand_vis), (coord, cand_coord))):
+        rows = pl.ds(3 * j, 3)
+        pairs = ((vis.at[0, j], cand_vis.at[j]), (coord.at[rows], cand_coord.at[rows]))
+        for n, (src, dst) in enumerate(pairs):
             moves.append(
                 pltpu.make_async_remote_copy(
-                    src_ref=src.at[0, j],
-                    dst_ref=dst.at[j],
+                    src_ref=src,
+                    dst_ref=dst,
                     send_sem=move_send.at[j, n],
                     recv_sem=move_recv.at[j, n],
                     device_id=to,
@@ -385,6 +385,15 @@
                 )
             )
             moves[-1].start()
+    for delta in ((3, 0, 3), (3, 0, 1), (1, 0, 3)):
+        tell(plane_sem, shifted(f, delta, 1), q)
+    pl.semaphore_wait(plane_sem, 3)
+    tell(near_sem, shifted(f, (0, 1, 0), 1), q)
+    for n in range(1, N_FREQ):
+        tell(near_sem, *peers_of(n))
+    pl.semaphore_wait(near_sem, N_FREQ)
+    for n in range(1, N_FREQ):
+        tell(all_sem, *peers_of(n))
     for c in own:
         c.wait()
     for c in moves:
@@ -408,21 +417,16 @@
         return pltpu.make_async_copy(res.at[n, f], dst.at[at, q], sem.at[at, q])
 
     def send_all(n):
-        def step(d, carry):
-            facet = (f + d) % N_FACET
-            here = jnp.logical_and(facet == f, group == q)
-
-            @pl.when(jnp.logical_not(here))
-            def _():
-                result_copy(n, facet).start()
-
-            @pl.when(here)
-            def _():
-                own_copy(n).start()
-
-            return carry
-
-        lax.fori_loop(0, N_FACET, step, 0)
+        for delta in SEND_ORDER:
+            result_copy(n, shifted(f, delta, 1)).start()
+
+        @pl.when(group != q)
+        def _():
+            result_copy(n, f).start()
+
+        @pl.when(group == q)
+        def _():
+            own_copy(n).start()
 
     def drain(n):
         def step(facet, carry):
@@ -440,7 +444,7 @@
         for j in range(1, BPC):
             block = jnp.where(shifted(f, DELTA[j], -1) == owner, j, block)
         unit_products(
-            q, block, cand_vis, cand_coord, corners[0, owner, block], corners[1, owner, block],
+            q, block, cand_vis, cand_coord, corners[block, 0, owner], corners[block, 1, owner],
             xrow, pbuf, vbuf, acc,
         )
 
@@ -451,6 +455,7 @@
 
         @pl.when(n == 0)
         def _():
+            pl.semaphore_wait(all_sem, N_FREQ - 1)
             send_all(0)
 
         @pl.when(n == 1)
@@ -466,6 +471,27 @@
     def settle(sem, dst, s):
         for p in range(N_FREQ):
             pltpu.make_async_copy(dst.at[s, p], dst.at[s, p], sem.at[s, p]).wait()
+
+    def share(at):
+        rows, copies = pl.ds(at, PER_SET), []
+        part = at // PER_SET
+        for n in range(1, N_FREQ):
+            copies.append(
+                pltpu.make_async_remote_copy(
+                    src_ref=total.at[rows],
+                    dst_ref=got.at[pl.ds(q * SLOTS + at, PER_SET)],
+                    send_sem=peer_send.at[part, n],
+                    recv_sem=peer_recv.at[part, n],
+                    device_id=peers_of(n),
+                    device_id_type=MESH,
+                )
+            )
+            copies[-1].start()
+        keep = pltpu.make_async_copy(
+            total.at[rows], got.at[pl.ds(q * SLOTS + at, PER_SET)], peer_send.at[part, 0]
+        )
+        keep.start()
+        return copies, keep
 
     for s in range(8):
         settle(recv_a, from_a, s)
@@ -476,6 +502,7 @@
             j = MEMBERS[g][min(s, len(MEMBERS[g]) - 1)]
             at = jnp.where(wanted == g, shifted(other, DELTA[j], 1) // 4, at)
         total[s] = (from_a[at, 0] + from_a[at, 1]) + (from_a[at, 2] + from_a[at, 3])
+    first = share(0)
     wanted = (q + N_FREQ - group_at(LAST)) % N_FREQ
     for s in range(PER_SET):
         present = pick(wanted, [int(s < len(m)) for m in MEMBERS]) == 1
@@ -489,25 +516,15 @@
         def _():
             total[PER_SET + s] = jnp.zeros((16, 128), f32)
 
-    peers = []
-    for d in range(1, N_FREQ):
-        peers.append(
-            pltpu.make_async_remote_copy(
-                src_ref=total,
-                dst_ref=got.at[pl.ds(q * SLOTS, SLOTS)],
-                send_sem=peer_send.at[d],
-                recv_sem=peer_recv.at[d],
-                device_id=(f, (q + d) % N_FREQ),
-                device_id_type=MESH,
-            )
-        )
-        peers[-1].start()
-    keep = pltpu.make_async_copy(total, got.at[pl.ds(q * SLOTS, SLOTS)], peer_send.at[0])
-    keep.start()
-    keep.wait()
-    for d in range(1, N_FREQ):
-        source = (q + N_FREQ - d) % N_FREQ
-        pltpu.make_async_copy(total, got.at[pl.ds(source * SLOTS, SLOTS)], peer_recv.at[d]).wait()
+    second = share(PER_SET)
+    peers = first[0] + second[0]
+    for part, (_, keep) in enumerate((first, second)):
+        keep.wait()
+        for n in range(1, N_FREQ):
+            rows = pl.ds((q + N_FREQ - n) % N_FREQ * SLOTS + part * PER_SET, PER_SET)
+            pltpu.make_async_copy(
+                total.at[pl.ds(0, PER_SET)], got.at[rows], peer_recv.at[part, n]
+            ).wait()
     make_image(q, other, got, table, pre, pim, br, bi, zr, zi, out)
     for c in moves:
         c.wait_send()
@@ -521,9 +538,10 @@
 
 
 def on_device(visibilities, coords, corners, owners, assign, counts):
-    d, _ = image_table()
-    plain = image_table()[1]
+    d, plain = image_table()
     scale = 1.0 / (SUB * SUB * math.sqrt(2 * BPC * BLK * CHANS))
+    high = (d * scale).astype(bf16)
+    low = (d * scale - high.astype(np.float64)).astype(bf16)
     smem = pl.BlockSpec(memory_space=pltpu.SMEM)
     vmem = pl.BlockSpec(memory_space=pltpu.VMEM)
     hbm = pl.BlockSpec(memory_space=pl.ANY)
@@ -535,7 +553,7 @@
         out_specs=vmem,
         scratch_shapes=[
             pltpu.VMEM((BPC, 2, CH, BLK), f32),
-            pltpu.VMEM((BPC, 3, BLK), f32),
+            pltpu.VMEM((3 * BPC, 1, BLK), f32),
         ]
         + unit_scratch()
         + [
@@ -550,24 +568,27 @@
             pltpu.VMEM((2, 640, G), bf16),
             pltpu.VMEM((32, 640), f32),
             pltpu.VMEM((32, 640), f32),
+            pltpu.SemaphoreType.REGULAR,
+            pltpu.SemaphoreType.REGULAR,
+            pltpu.SemaphoreType.REGULAR,
             dma((BPC, 2)),
             dma((BPC, 2)),
             dma((2, N_FACET)),
             dma((8, N_FREQ)),
             dma((PER_SET, N_FREQ)),
-            dma((N_FREQ,)),
-            dma((N_FREQ,)),
+            dma((2, N_FREQ)),
+            dma((2, N_FREQ)),
         ],
         compiler_params=pltpu.CompilerParams(collective_id=0, has_side_effects=True),
         name="grid_and_image",
     )(
         visibilities,
-        coords,
+        jnp.transpose(coords, (1, 2, 0, 3)).reshape(3 * BPC, 1, BLK),
         owners,
-        corners,
+        jnp.transpose(corners, (2, 0, 1)),
         assign,
         counts,
-        jnp.asarray(d * scale, f32),
+        jnp.asarray(np.concatenate([high, high, low], axis=1)),
         jnp.asarray(plain.T, f32),
     )
 

time: 39.8 us -> 32.5 us (0.82)
  Pallas kernels: 35.2 us -> 30 us
  local copies, waits for them, and re-layouts: 3.7 us -> 1.67 us
    pallas_call x1, Pallas kernels: 35.2 us -> 30 us  [on_device(): pl.pallas_call(fused_kernel, out_shape=jax.ShapeDtypeStruct((1, G // N_FR...]
    unnamed x5 -> x1, local copies, waits for them, and re-layouts: 3.7 us -> 1.67 us
where the time goes in v1:
time: 32.5 us; the launch traced here: 32.3 us
  Pallas kernels  30 us (92%)
  local copies, waits for them, and re-layouts  1.67 us (5%)
  between operations  0.66 us (2%)
    pallas_call x1, Pallas kernels, on_device(): pl.pallas_call(fused_kernel, out_shape=jax.ShapeDtypeStruct((1, G // N_FR...  30 us
    unnamed x1, local copies, waits for them, and re-layouts  1.67 us

profile of v1, /device:TPU:1, one launch (start us, length us, event | category | flops | bytes accessed | tf_op | source)
XLA Modules:
  0.0 32.3 jit_solution(2067829782992099898)
XLA Ops:
  0.7 30.0 %grid_and_image.1 = f32[1,128,512]{2,1,0:T(8,128)} custom-call(f32[1,10,2,32,128]{4,3,2,1,0:T(8,128)} %vis.1, f32[30,1,128]{2,1,0:T(1,128)} %bitcast.2, s32[2]{0:T(128)} %owners.1, s32[10,2,32]{2,1,0:T(2,128)} %bitcast.3, s32[1,20]{1,0:T(1,128)} %assign.1, s32[1]{0:T(128)S(6)} %copy.10.counts, bf16[512,96]{1,0:T(8,128)(2,1)} %constant.4.clone.table, ...), custom_call_target="tpu_custom_call" | custom-call | tf_op jit(solution)/shard_map/grid_and_image/pallas_call | solution.py:549
  30.7 1.7 %copy.11 = f32[1,128,512]{2,1,0:T(8,128)} copy(f32[1,128,512]{2,1,0:T(8,128)} %grid_and_image.1) | data formatting | bytes 524288

commit v2 on v1

--- a/solution.py
+++ b/solution.py
@@ -38,6 +38,8 @@
 LAST = N_FACET - 1
 PER_SET = 3
 SLOTS = 2 * PER_SET
+PADDED = 12
+WIDE = PADDED * SUB
 
 
 def fit_sincos():
@@ -251,41 +253,45 @@
 def lanes_of(values):
     group = lax.broadcasted_iota(jnp.int32, (1, 128), 1) // 32
     tiles = []
-    for tile in range(5):
+    for tile in range(PADDED // 4):
         v = jnp.full((1, 128), values[tile * 4], jnp.int32)
         for g in range(1, 4):
-            v = jnp.where(group == g, values[tile * 4 + g], v)
+            v = jnp.where(group == g, values[min(tile * 4 + g, BPC - 1)], v)
         tiles.append(v)
     return jnp.concatenate(tiles, axis=1)
 
 
 def prepare_image(q, owners, corners, assign, counts, other, table_t, pre, pim, br, bi):
     first_last = owners[0] == LAST
-    corner_u = [corners[j, 0, LAST] for j in range(BPC)] + [corners[j, 0, other] for j in range(BPC)]
-    corner_v = [corners[j, 1, LAST] for j in range(BPC)] + [corners[j, 1, other] for j in range(BPC)]
-    k_of = lax.broadcasted_iota(jnp.int32, (1, 640), 1) // 32
-    block = jnp.where(first_last, k_of, jnp.where(k_of < BPC, k_of + BPC, k_of - BPC))
-    weight = jnp.zeros((1, 640), f32)
     count = counts[0]
-    for n in range(2 * BPC):
-        live = jnp.where(n < count, 1.0, 0.0).astype(f32)
-        weight = weight + jnp.where(block == assign[0, n], live, 0.0)
-    rows = q * 128 - 256 + lax.broadcasted_iota(jnp.int32, (128, 640), 0)
-    turns = jnp.bitwise_and(rows * (2 * lanes_of(corner_u) - 481), 1023)
-    c, s = sincos(turns.astype(f32) * (1.0 / 1024.0))
-    pre[...] = c * weight
-    pim[...] = s * weight
+    k_of = lax.broadcasted_iota(jnp.int32, (1, WIDE), 1) // 32
+    rows = q * 128 - 256 + lax.broadcasted_iota(jnp.int32, (128, WIDE), 0)
     columns = lax.broadcasted_iota(jnp.int32, (1, G), 1) - 256
-    for k in range(2 * BPC):
-        turns = jnp.bitwise_and(columns * (2 * corner_v[k] - 481), 1023)
+    for part, owner in enumerate((other, LAST)):
+        base = jnp.where(first_last, BPC, 0) if part == 0 else jnp.where(first_last, 0, BPC)
+        block = jnp.where(k_of < BPC, base + k_of, -1)
+        weight = jnp.zeros((1, WIDE), f32)
+        for n in range(2 * BPC):
+            live = jnp.where(n < count, 1.0, 0.0).astype(f32)
+            weight = weight + jnp.where(block == assign[0, n], live, 0.0)
+        corner_u = lanes_of([corners[j, 0, owner] for j in range(BPC)])
+        turns = jnp.bitwise_and(rows * (2 * corner_u - 481), 1023)
         c, s = sincos(turns.astype(f32) * (1.0 / 1024.0))
-        for ref, value in ((br, table_t[...] * c), (bi, table_t[...] * -s)):
-            high, low = split(value)
-            ref[0, k * 32 : (k + 1) * 32, :] = high
-            ref[1, k * 32 : (k + 1) * 32, :] = low
-
-
-def make_image(q, other, got, table, pre, pim, br, bi, zr, zi, out):
+        pre[part] = c * weight
+        pim[part] = s * weight
+        for k in range(BPC):
+            turns = jnp.bitwise_and(columns * (2 * corners[k, 1, owner] - 481), 1023)
+            c, s = sincos(turns.astype(f32) * (1.0 / 1024.0))
+            for ref, value in ((br, table_t[...] * c), (bi, table_t[...] * -s)):
+                high, low = split(value)
+                ref[part, 0, k * 32 : (k + 1) * 32, :] = high
+                ref[part, 1, k * 32 : (k + 1) * 32, :] = low
+        for ref in (br, bi):
+            for h in range(2):
+                ref[part, h, BPC * 32 : WIDE, :] = jnp.zeros((WIDE - BPC * 32, G), bf16)
+
+
+def image_part(part, q, other, got, table, pre, pim, br, bi, zr, zi):
     lane = lax.broadcasted_iota(jnp.int32, (8, 128), 1)
     sub = lax.broadcasted_iota(jnp.int32, (8, 128), 0)
     row_sine = (sub // 4 + (sub // 2) % 2 + sub % 2) % 2 == 1
@@ -293,16 +299,18 @@
     two = jnp.logical_and(row_sine, lane_sine)
     one = jnp.logical_and(jnp.logical_or(row_sine, lane_sine), jnp.logical_not(two))
     group = lane // 32
-    home = group_at(other)
-    for tile in range(5):
+    home = group_at(other if part == 0 else LAST)
+    nothing = jnp.zeros((8, 128), f32)
+    for tile in range(PADDED // 4):
         parts = [[None] * 4, [None] * 4]
         for g in range(4):
-            k = tile * 4 + g
-            j = k % BPC
-            if k < BPC:
-                block = got[(group_at(LAST) + GROUP[j]) % N_FREQ * SLOTS + PER_SET + RANK[j]]
-            else:
-                block = got[(home + GROUP[j]) % N_FREQ * SLOTS + RANK[j]]
+            j = tile * 4 + g
+            if j >= BPC:
+                for i4 in range(4):
+                    for p in range(2):
+                        parts[p][i4] = jnp.where(group == g, nothing, parts[p][i4])
+                continue
+            block = got[(home + GROUP[j]) % N_FREQ * PER_SET + RANK[j]]
             re, im = block[:8], block[8:]
             new_re = jnp.where(one, -im, jnp.where(two, -re, re))
             new_im = jnp.where(one, re, jnp.where(two, -im, im))
@@ -325,16 +333,19 @@
         )
 
     t_re, t_im = apply(zr[...]), apply(zi[...])
-    l_re = t_re * pre[...] - t_im * pim[...]
-    l_im = t_re * pim[...] + t_im * pre[...]
-    out[0] = dot3(split(l_re), (br[0], br[1])) + dot3(split(l_im), (bi[0], bi[1]))
+    l_re = t_re * pre[part] - t_im * pim[part]
+    l_im = t_re * pim[part] + t_im * pre[part]
+    return dot3(split(l_re), (br[part, 0], br[part, 1])) + dot3(
+        split(l_im), (bi[part, 0], bi[part, 1])
+    )
 
 
 def fused_kernel(
-    vis, coord, owners, corners, assign, counts, table, table_t, out,
-    cand_vis, cand_coord, xrow, pbuf, vbuf, acc, turned, res, from_a, from_b, total, got,
+    vis, coord, owners_in, corners_in, assign_in, counts_in, table_in, table_t_in, out,
+    owners, corners, assign, counts, table, table_t,
+    cand_vis, cand_coord, xrow, pbuf, vbuf, acc, turned, res, from_a, from_b, total, got_a, got_b,
     pre, pim, br, bi, zr, zi,
-    plane_sem, near_sem, all_sem, move_send, move_recv, send_sem, recv_a, recv_b, peer_send, peer_recv,
+    plane_sem, near_sem, all_sem, args_sem, move_send, move_recv, send_sem, recv_a, recv_b, peer_send, peer_recv,
 ):
     f = lax.axis_index("facet")
     q = lax.axis_index("freq")
@@ -344,7 +355,6 @@
         last_block = jnp.where(f == LAST_POS[j], j, last_block)
     is_last = last_block >= 0
     last_rank = pick(last_block, RANK)
-    other = jnp.where(owners[0] == LAST, owners[1], owners[0]).astype(jnp.int32)
     barrier = pltpu.get_barrier_semaphore()
 
     def signal(facet, freq):
@@ -361,11 +371,24 @@
     def tell(sem, facet, freq):
         pl.semaphore_signal(sem, inc=1, device_id=(facet, freq), device_id_type=MESH)
 
+    args = [
+        pltpu.make_async_copy(src, dst, args_sem.at[n])
+        for n, (src, dst) in enumerate(
+            (
+                (owners_in, owners),
+                (corners_in, corners),
+                (assign_in, assign),
+                (counts_in, counts),
+                (table_in, table),
+                (table_t_in, table_t),
+            )
+        )
+    ]
     own = [
         pltpu.make_async_copy(vis.at[0, 0], cand_vis.at[0], move_recv.at[0, 0]),
         pltpu.make_async_copy(coord.at[pl.ds(0, 3)], cand_coord.at[pl.ds(0, 3)], move_recv.at[0, 1]),
     ]
-    for c in own:
+    for c in own + args:
         c.start()
     pl.semaphore_wait(barrier, BPC - 1 + N_FREQ - 1)
     moves = []
@@ -394,11 +417,12 @@
     pl.semaphore_wait(near_sem, N_FREQ)
     for n in range(1, N_FREQ):
         tell(all_sem, *peers_of(n))
-    for c in own:
+    for c in own + args:
         c.wait()
     for c in moves:
         c.wait_recv()
 
+    other = jnp.where(owners[0] == LAST, owners[1], owners[0]).astype(jnp.int32)
     place = f // 4
 
     def result_copy(n, facet):
@@ -472,14 +496,13 @@
         for p in range(N_FREQ):
             pltpu.make_async_copy(dst.at[s, p], dst.at[s, p], sem.at[s, p]).wait()
 
-    def share(at):
-        rows, copies = pl.ds(at, PER_SET), []
-        part = at // PER_SET
-        for n in range(1, N_FREQ):
+    def share(got, at, size, part):
+        rows, copies = pl.ds(at, size), []
+        for n in (2, 1, 3):
             copies.append(
                 pltpu.make_async_remote_copy(
                     src_ref=total.at[rows],
-                    dst_ref=got.at[pl.ds(q * SLOTS + at, PER_SET)],
+                    dst_ref=got.at[pl.ds(q * PER_SET + at % PER_SET, size)],
                     send_sem=peer_send.at[part, n],
                     recv_sem=peer_recv.at[part, n],
                     device_id=peers_of(n),
@@ -488,10 +511,18 @@
             )
             copies[-1].start()
         keep = pltpu.make_async_copy(
-            total.at[rows], got.at[pl.ds(q * SLOTS + at, PER_SET)], peer_send.at[part, 0]
+            total.at[rows], got.at[pl.ds(q * PER_SET + at % PER_SET, size)], peer_send.at[part, 0]
         )
         keep.start()
         return copies, keep
+
+    def collect(got, shared, at, size, part):
+        shared[1].wait()
+        for n in range(1, N_FREQ):
+            rows = pl.ds((q + N_FREQ - n) % N_FREQ * PER_SET + at % PER_SET, size)
+            pltpu.make_async_copy(
+                total.at[pl.ds(0, size)], got.at[rows], peer_recv.at[part, n]
+            ).wait()
 
     for s in range(8):
         settle(recv_a, from_a, s)
@@ -502,7 +533,8 @@
             j = MEMBERS[g][min(s, len(MEMBERS[g]) - 1)]
             at = jnp.where(wanted == g, shifted(other, DELTA[j], 1) // 4, at)
         total[s] = (from_a[at, 0] + from_a[at, 1]) + (from_a[at, 2] + from_a[at, 3])
-    first = share(0)
+    first = share(got_a, 0, PER_SET, 0)
+    later = []
     wanted = (q + N_FREQ - group_at(LAST)) % N_FREQ
     for s in range(PER_SET):
         present = pick(wanted, [int(s < len(m)) for m in MEMBERS]) == 1
@@ -516,16 +548,15 @@
         def _():
             total[PER_SET + s] = jnp.zeros((16, 128), f32)
 
-    second = share(PER_SET)
-    peers = first[0] + second[0]
-    for part, (_, keep) in enumerate((first, second)):
-        keep.wait()
-        for n in range(1, N_FREQ):
-            rows = pl.ds((q + N_FREQ - n) % N_FREQ * SLOTS + part * PER_SET, PER_SET)
-            pltpu.make_async_copy(
-                total.at[pl.ds(0, PER_SET)], got.at[rows], peer_recv.at[part, n]
-            ).wait()
-    make_image(q, other, got, table, pre, pim, br, bi, zr, zi, out)
+        later.append(share(got_b, PER_SET + s, 1, 1 + s))
+
+    peers = first[0]
+    collect(got_a, first, 0, PER_SET, 0)
+    out[0] = image_part(0, q, other, got_a, table, pre, pim, br, bi, zr, zi)
+    for s, shared in enumerate(later):
+        peers = peers + shared[0]
+        collect(got_b, shared, PER_SET + s, 1, 1 + s)
+    out[0] = out[0] + image_part(1, q, other, got_b, table, pre, pim, br, bi, zr, zi)
     for c in moves:
         c.wait_send()
     for p in peers:
@@ -542,16 +573,21 @@
     scale = 1.0 / (SUB * SUB * math.sqrt(2 * BPC * BLK * CHANS))
     high = (d * scale).astype(bf16)
     low = (d * scale - high.astype(np.float64)).astype(bf16)
-    smem = pl.BlockSpec(memory_space=pltpu.SMEM)
     vmem = pl.BlockSpec(memory_space=pltpu.VMEM)
     hbm = pl.BlockSpec(memory_space=pl.ANY)
     dma = pltpu.SemaphoreType.DMA
     return pl.pallas_call(
         fused_kernel,
-        out_shape=jax.ShapeDtypeStruct((1, G // N_FREQ, G), f32),
-        in_specs=[hbm, hbm] + [smem] * 4 + [vmem] * 2,
+        out_shape=pltpu.VMEM((1, G // N_FREQ, G), f32),
+        in_specs=[hbm] * 8,
         out_specs=vmem,
         scratch_shapes=[
+            pltpu.SMEM((2,), jnp.int32),
+            pltpu.SMEM((BPC, 2, N_FACET), jnp.int32),
+            pltpu.SMEM((1, 2 * BPC), jnp.int32),
+            pltpu.SMEM((1,), jnp.int32),
+            pltpu.VMEM((G, 3 * SUB), bf16),
+            pltpu.VMEM((SUB, G), f32),
             pltpu.VMEM((BPC, 2, CH, BLK), f32),
             pltpu.VMEM((3 * BPC, 1, BLK), f32),
         ]
@@ -561,23 +597,25 @@
             pltpu.VMEM((8, N_FREQ, 16, 128), f32),
             pltpu.VMEM((PER_SET, N_FREQ, 16, 128), f32),
             pltpu.VMEM((SLOTS, 16, 128), f32),
-            pltpu.VMEM((N_FREQ * SLOTS, 16, 128), f32),
-            pltpu.VMEM((128, 640), f32),
-            pltpu.VMEM((128, 640), f32),
-            pltpu.VMEM((2, 640, G), bf16),
-            pltpu.VMEM((2, 640, G), bf16),
-            pltpu.VMEM((32, 640), f32),
-            pltpu.VMEM((32, 640), f32),
+            pltpu.VMEM((N_FREQ * PER_SET, 16, 128), f32),
+            pltpu.VMEM((N_FREQ * PER_SET, 16, 128), f32),
+            pltpu.VMEM((2, 128, WIDE), f32),
+            pltpu.VMEM((2, 128, WIDE), f32),
+            pltpu.VMEM((2, 2, WIDE, G), bf16),
+            pltpu.VMEM((2, 2, WIDE, G), bf16),
+            pltpu.VMEM((32, WIDE), f32),
+            pltpu.VMEM((32, WIDE), f32),
             pltpu.SemaphoreType.REGULAR,
             pltpu.SemaphoreType.REGULAR,
             pltpu.SemaphoreType.REGULAR,
+            dma((6,)),
             dma((BPC, 2)),
             dma((BPC, 2)),
             dma((2, N_FACET)),
             dma((8, N_FREQ)),
             dma((PER_SET, N_FREQ)),
-            dma((2, N_FREQ)),
-            dma((2, N_FREQ)),
+            dma((1 + PER_SET, N_FREQ)),
+            dma((1 + PER_SET, N_FREQ)),
         ],
         compiler_params=pltpu.CompilerParams(collective_id=0, has_side_effects=True),
         name="grid_and_image",

time: 32.5 us -> 29.8 us (0.917)
  Pallas kernels: 30 us -> 28.2 us
  local copies, waits for them, and re-layouts: 1.67 us -> 0.71 us
    pallas_call x1, Pallas kernels: 30 us -> 28.2 us  [on_device(): pl.pallas_call(fused_kernel, out_shape=pltpu.VMEM((1, G // N_FREQ, G), f3...]
    unnamed x1, local copies, waits for them, and re-layouts: 1.67 us -> 0.71 us
where the time goes in v2:
time: 29.8 us; the launch traced here: 29.5 us
  Pallas kernels  28.2 us (95%)
  local copies, waits for them, and re-layouts  0.71 us (2%)
  between operations  0.66 us (2%)
    pallas_call x1, Pallas kernels, on_device(): pl.pallas_call(fused_kernel, out_shape=pltpu.VMEM((1, G // N_FREQ, G), f3...  28.2 us
    unnamed x1, local copies, waits for them, and re-layouts  0.71 us

profile of v2, /device:TPU:1, one launch (start us, length us, event | category | flops | bytes accessed | tf_op | source)
XLA Modules:
  0.0 29.5 jit_solution(7891662116281177347)
XLA Ops:
  0.7 28.2 %grid_and_image.1 = f32[1,128,512]{2,1,0:T(8,128)S(1)} custom-call(f32[1,10,2,32,128]{4,3,2,1,0:T(8,128)} %vis.1, f32[30,1,128]{2,1,0:T(1,128)} %bitcast.2, s32[2]{0:T(128)} %owners_in.1, s32[10,2,32]{2,1,0:T(2,128)} %bitcast.3, s32[1,20]{1,0:T(1,128)} %assign_in.1, s32[1]{0:T(128)S(6)} %copy.11.counts_in, bf16[512,96]{1,0:T(8,128)(2,1)} %constant.4.clone.table_in, ...), custom_call_target="tpu_custom_call" | custom-call | tf_op jit(solution)/shard_map/grid_and_image/pallas_call | solution.py:579
  28.8 0.7 %copy.10 = f32[1,128,512]{2,1,0:T(8,128)} copy(f32[1,128,512]{2,1,0:T(8,128)S(1)} %grid_and_image.1) | data formatting | bytes 524288

commit v3 on v2

--- a/solution.py
+++ b/solution.py
@@ -102,12 +102,16 @@
     return table, plain
 
 
-def shifted(f, delta, sign):
-    z, y, x = f // 8, (f // 4) % 2, f % 4
-    z = (z + (delta[0] if sign > 0 else 4 - delta[0])) % 4
-    y = (y + delta[1]) % 2
-    x = (x + (delta[2] if sign > 0 else 4 - delta[2])) % 4
-    return z * 8 + y * 4 + x
+def around(f):
+    z, y, x = lax.div(f, 8), lax.rem(lax.div(f, 4), 2), lax.rem(f, 4)
+    zs = [lax.rem(z + d, 4) * 8 for d in range(4)]
+    ys = [lax.rem(y + d, 2) * 4 for d in range(2)]
+    xs = [lax.rem(x + d, 4) for d in range(4)]
+
+    def go(delta, sign):
+        return zs[sign * delta[0] % 4] + ys[delta[1]] + xs[sign * delta[2] % 4]
+
+    return go
 
 
 def shifted_int(f, delta):
@@ -119,7 +123,9 @@
 
 
 def group_at(f):
-    return group_of(f // 8, (f // 4) % 2, f % 4)
+    if isinstance(f, int):
+        return group_of(f // 8, f // 4 % 2, f % 4)
+    return lax.rem(lax.div(f, 8) + lax.rem(f, 4) + 2 * lax.rem(lax.div(f, 4), 2), N_FREQ)
 
 
 GROUP = tuple(group_of(*d) for d in DELTA)
@@ -310,7 +316,7 @@
                     for p in range(2):
                         parts[p][i4] = jnp.where(group == g, nothing, parts[p][i4])
                 continue
-            block = got[(home + GROUP[j]) % N_FREQ * PER_SET + RANK[j]]
+            block = got[((home + GROUP[j]) % N_FREQ if part else lax.rem(home + GROUP[j], N_FREQ)) * PER_SET + RANK[j]]
             re, im = block[:8], block[8:]
             new_re = jnp.where(one, -im, jnp.where(two, -re, re))
             new_im = jnp.where(one, re, jnp.where(two, -im, im))
@@ -349,6 +355,7 @@
 ):
     f = lax.axis_index("facet")
     q = lax.axis_index("freq")
+    here = around(f)
     group = group_at(f)
     last_block = jnp.int32(-1)
     for j in range(BPC):
@@ -361,10 +368,10 @@
         pl.semaphore_signal(barrier, inc=1, device_id=(facet, freq), device_id_type=MESH)
 
     def peers_of(n):
-        return (f, (q + n) % N_FREQ)
+        return (f, lax.rem(q + n, N_FREQ))
 
     for j in range(1, BPC):
-        signal(shifted(f, DELTA[j], -1), q)
+        signal(here(DELTA[j], -1), q)
     for n in range(1, N_FREQ):
         signal(*peers_of(n))
 
@@ -393,7 +400,7 @@
     pl.semaphore_wait(barrier, BPC - 1 + N_FREQ - 1)
     moves = []
     for j in range(BPC - 1, 0, -1):
-        to = (shifted(f, DELTA[j], 1), q)
+        to = (here(DELTA[j], 1), q)
         rows = pl.ds(3 * j, 3)
         pairs = ((vis.at[0, j], cand_vis.at[j]), (coord.at[rows], cand_coord.at[rows]))
         for n, (src, dst) in enumerate(pairs):
@@ -409,9 +416,9 @@
             )
             moves[-1].start()
     for delta in ((3, 0, 3), (3, 0, 1), (1, 0, 3)):
-        tell(plane_sem, shifted(f, delta, 1), q)
+        tell(plane_sem, here(delta, 1), q)
     pl.semaphore_wait(plane_sem, 3)
-    tell(near_sem, shifted(f, (0, 1, 0), 1), q)
+    tell(near_sem, here((0, 1, 0), 1), q)
     for n in range(1, N_FREQ):
         tell(near_sem, *peers_of(n))
     pl.semaphore_wait(near_sem, N_FREQ)
@@ -423,26 +430,27 @@
         c.wait_recv()
 
     other = jnp.where(owners[0] == LAST, owners[1], owners[0]).astype(jnp.int32)
-    place = f // 4
+    there = around(other)
+    place = lax.div(f, 4)
 
     def result_copy(n, facet):
         dst, sem, at = (from_a, recv_a, place) if n == 0 else (from_b, recv_b, last_rank)
         return pltpu.make_async_remote_copy(
             src_ref=res.at[n, facet],
             dst_ref=dst.at[at, q],
-            send_sem=send_sem.at[n, facet],
-            recv_sem=sem.at[at, q],
+            send_sem=send_sem.at[n],
+            recv_sem=sem.at[at] if n else sem,
             device_id=(facet, group),
             device_id_type=MESH,
         )
 
     def own_copy(n):
         dst, sem, at = (from_a, recv_a, place) if n == 0 else (from_b, recv_b, last_rank)
-        return pltpu.make_async_copy(res.at[n, f], dst.at[at, q], sem.at[at, q])
+        return pltpu.make_async_copy(res.at[n, f], dst.at[at, q], sem.at[at] if n else sem)
 
     def send_all(n):
         for delta in SEND_ORDER:
-            result_copy(n, shifted(f, delta, 1)).start()
+            result_copy(n, here(delta, 1)).start()
 
         @pl.when(group != q)
         def _():
@@ -453,20 +461,20 @@
             own_copy(n).start()
 
     def drain(n):
-        def step(facet, carry):
-            @pl.when(jnp.logical_not(jnp.logical_and(facet == f, group == q)))
-            def _():
-                result_copy(n, facet).wait_send()
-
-            return carry
-
-        lax.fori_loop(0, N_FACET, step, 0)
+        @pl.when(group != q)
+        def _():
+            pltpu.make_async_copy(res.at[n], res.at[n], send_sem.at[n]).wait()
+
+        @pl.when(group == q)
+        def _():
+            sent = res.at[n, pl.ds(0, N_FACET - 1)]
+            pltpu.make_async_copy(sent, sent, send_sem.at[n]).wait()
 
     def unit(n, carry):
         owner = jnp.where(n == 1, LAST, other)
         block = jnp.int32(0)
         for j in range(1, BPC):
-            block = jnp.where(shifted(f, DELTA[j], -1) == owner, j, block)
+            block = jnp.where(here(DELTA[j], -1) == owner, j, block)
         unit_products(
             q, block, cand_vis, cand_coord, corners[block, 0, owner], corners[block, 1, owner],
             xrow, pbuf, vbuf, acc,
@@ -490,11 +498,9 @@
 
     lax.fori_loop(0, 1 + jnp.where(is_last, 1, 0), unit, 0)
 
+    for c in moves:
+        c.wait_send()
     prepare_image(q, owners, corners, assign, counts, other, table_t, pre, pim, br, bi)
-
-    def settle(sem, dst, s):
-        for p in range(N_FREQ):
-            pltpu.make_async_copy(dst.at[s, p], dst.at[s, p], sem.at[s, p]).wait()
 
     def share(got, at, size, part):
         rows, copies = pl.ds(at, size), []
@@ -519,29 +525,28 @@
     def collect(got, shared, at, size, part):
         shared[1].wait()
         for n in range(1, N_FREQ):
-            rows = pl.ds((q + N_FREQ - n) % N_FREQ * PER_SET + at % PER_SET, size)
+            rows = pl.ds(lax.rem(q + N_FREQ - n, N_FREQ) * PER_SET + at % PER_SET, size)
             pltpu.make_async_copy(
                 total.at[pl.ds(0, size)], got.at[rows], peer_recv.at[part, n]
             ).wait()
 
-    for s in range(8):
-        settle(recv_a, from_a, s)
-    wanted = (q + N_FREQ - group_at(other)) % N_FREQ
+    pltpu.make_async_copy(from_a, from_a, recv_a).wait()
+    wanted = lax.rem(q + N_FREQ - group_at(other), N_FREQ)
     for s in range(PER_SET):
         at = jnp.int32(0)
         for g in range(N_FREQ):
             j = MEMBERS[g][min(s, len(MEMBERS[g]) - 1)]
-            at = jnp.where(wanted == g, shifted(other, DELTA[j], 1) // 4, at)
+            at = jnp.where(wanted == g, lax.div(there(DELTA[j], 1), 4), at)
         total[s] = (from_a[at, 0] + from_a[at, 1]) + (from_a[at, 2] + from_a[at, 3])
     first = share(got_a, 0, PER_SET, 0)
     later = []
-    wanted = (q + N_FREQ - group_at(LAST)) % N_FREQ
+    wanted = lax.rem(q + N_FREQ - group_at(LAST), N_FREQ)
     for s in range(PER_SET):
         present = pick(wanted, [int(s < len(m)) for m in MEMBERS]) == 1
 
         @pl.when(present)
         def _():
-            settle(recv_b, from_b, s)
+            pltpu.make_async_copy(from_b.at[s], from_b.at[s], recv_b.at[s]).wait()
             total[PER_SET + s] = (from_b[s, 0] + from_b[s, 1]) + (from_b[s, 2] + from_b[s, 3])
 
         @pl.when(jnp.logical_not(present))
@@ -557,8 +562,6 @@
         peers = peers + shared[0]
         collect(got_b, shared, PER_SET + s, 1, 1 + s)
     out[0] = out[0] + image_part(1, q, other, got_b, table, pre, pim, br, bi, zr, zi)
-    for c in moves:
-        c.wait_send()
     for p in peers:
         p.wait_send()
     drain(0)
@@ -611,9 +614,9 @@
             dma((6,)),
             dma((BPC, 2)),
             dma((BPC, 2)),
-            dma((2, N_FACET)),
-            dma((8, N_FREQ)),
-            dma((PER_SET, N_FREQ)),
+            dma((2,)),
+            dma,
+            dma((PER_SET,)),
             dma((1 + PER_SET, N_FREQ)),
             dma((1 + PER_SET, N_FREQ)),
         ],

time: 29.8 us -> 28.6 us (0.960)
  Pallas kernels: 28.2 us -> 26.9 us
    pallas_call x1, Pallas kernels: 28.2 us -> 26.9 us  [on_device(): pl.pallas_call(fused_kernel, out_shape=pltpu.VMEM((1, G // N_FREQ, G), f3...]
where the time goes in v3:
time: 28.6 us; the launch traced here: 28.3 us
  Pallas kernels  26.9 us (94%)
  local copies, waits for them, and re-layouts  0.71 us (2%)
  between operations  0.66 us (2%)
    pallas_call x1, Pallas kernels, on_device(): pl.pallas_call(fused_kernel, out_shape=pltpu.VMEM((1, G // N_FREQ, G), f3...  26.9 us
    unnamed x1, local copies, waits for them, and re-layouts  0.71 us

profile of v3, /device:TPU:1, one launch (start us, length us, event | category | flops | bytes accessed | tf_op | source)
XLA Modules:
  0.0 28.3 jit_solution(16214818765809495283)
XLA Ops:
  0.7 26.9 %grid_and_image.1 = f32[1,128,512]{2,1,0:T(8,128)S(1)} custom-call(f32[1,10,2,32,128]{4,3,2,1,0:T(8,128)} %vis.1, f32[30,1,128]{2,1,0:T(1,128)} %bitcast.2, s32[2]{0:T(128)} %owners_in.1, s32[10,2,32]{2,1,0:T(2,128)} %bitcast.3, s32[1,20]{1,0:T(1,128)} %assign_in.1, s32[1]{0:T(128)S(6)} %copy.11.counts_in, bf16[512,96]{1,0:T(8,128)(2,1)} %constant.4.clone.table_in, ...), custom_call_target="tpu_custom_call" | custom-call | tf_op jit(solution)/shard_map/grid_and_image/pallas_call | solution.py:582
  27.5 0.7 %copy.10 = f32[1,128,512]{2,1,0:T(8,128)} copy(f32[1,128,512]{2,1,0:T(8,128)S(1)} %grid_and_image.1) | data formatting | bytes 524288

commit v4 on v3

--- a/solution.py
+++ b/solution.py
@@ -17,7 +17,7 @@
 N_FREQ = 4
 BLK = 128
 CHANS = CH * N_FREQ
-CHUNK = 8
+CHUNK = 16
 LO = False
 MESH = pl.DeviceIdType.MESH
 f32 = jnp.float32

time: 28.6 us -> 28.4 us (level)
  no operation moved by 1% of the time
where the time goes in v4:
time: 28.4 us; the launch traced here: 28.3 us
  Pallas kernels  26.9 us (95%)
  local copies, waits for them, and re-layouts  0.71 us (2%)
  between operations  0.66 us (2%)
    pallas_call x1, Pallas kernels, on_device(): pl.pallas_call(fused_kernel, out_shape=pltpu.VMEM((1, G // N_FREQ, G), f3...  26.9 us
    unnamed x1, local copies, waits for them, and re-layouts  0.71 us

profile of v4, /device:TPU:1, one launch (start us, length us, event | category | flops | bytes accessed | tf_op | source)
XLA Modules:
  0.0 28.3 jit_solution(8109389786349415826)
XLA Ops:
  0.7 26.9 %grid_and_image.1 = f32[1,128,512]{2,1,0:T(8,128)S(1)} custom-call(f32[1,10,2,32,128]{4,3,2,1,0:T(8,128)} %vis.1, f32[30,1,128]{2,1,0:T(1,128)} %bitcast.2, s32[2]{0:T(128)} %owners_in.1, s32[10,2,32]{2,1,0:T(2,128)} %bitcast.3, s32[1,20]{1,0:T(1,128)} %assign_in.1, s32[1]{0:T(128)S(6)} %copy.11.counts_in, bf16[512,96]{1,0:T(8,128)(2,1)} %constant.4.clone.table_in, ...), custom_call_target="tpu_custom_call" | custom-call | tf_op jit(solution)/shard_map/grid_and_image/pallas_call | solution.py:582
  27.6 0.7 %copy.10 = f32[1,128,512]{2,1,0:T(8,128)} copy(f32[1,128,512]{2,1,0:T(8,128)S(1)} %grid_and_image.1) | data formatting | bytes 524288

commit v5 on v4

--- a/solution.py
+++ b/solution.py
@@ -370,7 +370,7 @@
     def peers_of(n):
         return (f, lax.rem(q + n, N_FREQ))
 
-    for j in range(1, BPC):
+    for j in range(BPC - 1, 0, -1):
         signal(here(DELTA[j], -1), q)
     for n in range(1, N_FREQ):
         signal(*peers_of(n))
@@ -558,17 +558,18 @@
     peers = first[0]
     collect(got_a, first, 0, PER_SET, 0)
     out[0] = image_part(0, q, other, got_a, table, pre, pim, br, bi, zr, zi)
+    drain(0)
+
+    @pl.when(is_last)
+    def _():
+        drain(1)
+
     for s, shared in enumerate(later):
         peers = peers + shared[0]
         collect(got_b, shared, PER_SET + s, 1, 1 + s)
-    out[0] = out[0] + image_part(1, q, other, got_b, table, pre, pim, br, bi, zr, zi)
     for p in peers:
         p.wait_send()
-    drain(0)
-
-    @pl.when(is_last)
-    def _():
-        drain(1)
+    out[0] = out[0] + image_part(1, q, other, got_b, table, pre, pim, br, bi, zr, zi)
 
 
 def on_device(visibilities, coords, corners, owners, assign, counts):

time: 28.4 us -> 28.3 us (level)
  no operation moved by 1% of the time
where the time goes in v5:
time: 28.3 us; the launch traced here: 28.2 us
  Pallas kernels  26.9 us (95%)
  local copies, waits for them, and re-layouts  0.71 us (3%)
  between operations  0.66 us (2%)
    pallas_call x1, Pallas kernels, on_device(): pl.pallas_call(fused_kernel, out_shape=pltpu.VMEM((1, G // N_FREQ, G), f3...  26.9 us
    unnamed x1, local copies, waits for them, and re-layouts  0.71 us

profile of v5, /device:TPU:1, one launch (start us, length us, event | category | flops | bytes accessed | tf_op | source)
XLA Modules:
  0.0 28.2 jit_solution(10159501499629947155)
XLA Ops:
  0.7 26.9 %grid_and_image.1 = f32[1,128,512]{2,1,0:T(8,128)S(1)} custom-call(f32[1,10,2,32,128]{4,3,2,1,0:T(8,128)} %vis.1, f32[30,1,128]{2,1,0:T(1,128)} %bitcast.2, s32[2]{0:T(128)} %owners_in.1, s32[10,2,32]{2,1,0:T(2,128)} %bitcast.3, s32[1,20]{1,0:T(1,128)} %assign_in.1, s32[1]{0:T(128)S(6)} %copy.11.counts_in, bf16[512,96]{1,0:T(8,128)(2,1)} %constant.4.clone.table_in, ...), custom_call_target="tpu_custom_call" | custom-call | tf_op jit(solution)/shard_map/grid_and_image/pallas_call | solution.py:583
  27.5 0.7 %copy.10 = f32[1,128,512]{2,1,0:T(8,128)} copy(f32[1,128,512]{2,1,0:T(8,128)S(1)} %grid_and_image.1) | data formatting | bytes 524288
